TPU v7x, 32 devices: a whole 2x2x4 slice. The times are simulated.
32 devices in a mesh: section: 2 (over y), expert: 8 (over z, x), dp: 2 (over core).
Axes of the slice: x: 2, y: 2, z: 4, core: 2. Of those that a mesh axis runs over, the one named last changes fastest.
Arguments:
- tokens_in: bfloat16 [8, 256, 2048], P(None, ('expert', 'dp')), may hold values from -6 to 6
- cotangent: bfloat16 [8, 256, 2048], P(None, ('expert', 'dp')), may hold values from -4 to 4
- routes: int32 [2, 8, 256, 8], P('section', None, ('expert', 'dp')), may hold values from 0 to 15, all different within a row; in each aligned block of 16 rows (0 to 15, 16 to 31, ..., all dimensions but the last counted through in order) at most 10 rows name the same one
- router_weights: float32 [2, 8, 256, 8], P('section', None, ('expert', 'dp')), may hold values from 0.1 to 0.6
- norm_gain: float32 [2, 2048], P('section'), may hold values from 0.25 to 1.75
- w_gate: bfloat16 [2, 16, 2048, 512], P('section', 'expert'), may hold values from -0.125 to 0.125
- w_up: bfloat16 [2, 16, 2048, 512], P('section', 'expert'), may hold values from -0.125 to 0.125
- w_down: bfloat16 [2, 16, 512, 2048], P('section', 'expert'), may hold values from -0.25 to 0.25
Outputs:
- layer_out: bfloat16 [2, 8, 256, 2048], P('section', None, ('expert', 'dp'))
- input_grad: bfloat16 [2, 8, 256, 2048], P('section', None, ('expert', 'dp'))
- grad_gate: bfloat16 [2, 16, 2048, 512], P('section', 'expert', 'dp')
- grad_up: bfloat16 [2, 16, 2048, 512], P('section', 'expert', 'dp')
- grad_down: bfloat16 [2, 16, 512, 2048], P('section', 'expert', 'dp')
Inputs may be any that keep to these rules, and one draw needn't show every extreme that they name: `routes`: each row names 8 different experts. In each aligned block of 16 rows (the tokens of one device for one layer and one micro-batch) no expert is named by more than 10 rows, and in some blocks one is named by exactly 10.
All inputs are finite; a program needn't handle non-finite values.
Results may differ from a plain program's by a relative error of at most 0.022.
Values may be sent and summed in bfloat16 or wider, within the bound.
A program may use at most 128 MiB of HBM per device.

v0:
```python
import jax
import jax.numpy as jnp
from jax import lax
from jax.sharding import PartitionSpec as P

epsilon = 1e-06
ROW_LIMIT = 1024


def from_behind(block, axis, distance):
    devices = range(lax.axis_size(axis))
    route = [(i - distance, i) for i in devices if i - distance in devices]
    return lax.ppermute(block, axis, route)


def pick(section_id, by_section):
    entries = list(by_section.items())
    chosen = entries[0][1]
    for section, value in entries[1:]:
        if value is not chosen:
            chosen = jnp.where(section_id == section, value, chosen)
    return chosen


def weight_table(route_ids, route_weights, experts, expert_count):
    labels = jnp.arange(experts, dtype=jnp.int32)[:, None, None, None]
    dense = jnp.sum(jnp.where(route_ids[None] == labels, route_weights[None], 0.0), axis=3)
    dense = dense.reshape((expert_count, experts // expert_count) + dense.shape[1:])
    return lax.all_to_all(dense, "expert", split_axis=0, concat_axis=0, tiled=True)


def on_device(tokens_in, cotangent, routes, router_weights, norm_gain, w_gate, w_up, w_down):
    micro_count, token_rows, width = tokens_in.shape
    held, hidden_units = (w_gate.shape[1], w_gate.shape[3])
    sections = lax.axis_size("section")
    expert_count = lax.axis_size("expert")
    dp_count = lax.axis_size("dp")
    chunks = 1
    while (
        micro_count % (2 * chunks) == 0
        and micro_count * token_rows * expert_count > ROW_LIMIT * chunks
    ):
        chunks *= 2
    per_chunk = micro_count // chunks
    own_rows = per_chunk * token_rows
    ticks = sections + chunks - 1
    inner = held * hidden_units
    section_id = lax.axis_index("section")
    gain_row = norm_gain[0]
    table = weight_table(routes[0], router_weights[0], held * expert_count, expert_count)
    w_in = jnp.concatenate(
        [w_gate[0, e] for e in range(held)] + [w_up[0, e] for e in range(held)], axis=1
    )
    w_out = w_down[0].reshape(inner, width)

    def chunk_of(array, chunk, axis):
        if chunks == 1:
            return array
        return lax.dynamic_slice_in_dim(array, chunk * per_chunk, per_chunk, axis)

    def spread_weights(chunk):
        rows = chunk_of(table, chunk, 2).transpose(0, 2, 3, 1).reshape(-1, held)
        return jnp.repeat(rows, hidden_units, axis=1)

    def gather(rows):
        return lax.all_gather(rows, "expert", axis=0, tiled=True)

    def scatter(rows):
        return lax.psum_scatter(rows, "expert", scatter_dimension=0, tiled=True)

    def rms(hidden):
        widened = hidden.astype(jnp.float32)
        return (widened, lax.rsqrt(jnp.mean(widened * widened, axis=-1, keepdims=True) + epsilon))

    compact = sections > 2

    def keep(store, value, owner):
        if not compact:
            store.append(value)
        elif not store:
            store.extend([value] * chunks)
        else:
            store[:] = [
                jnp.where(section_id == owner(c), value, old) for c, old in enumerate(store)
            ]
            store[:] = lax.optimization_barrier(store)

    def at(store, chunk, shift):
        return store[chunk] if compact else store[chunk + shift]

    hiddens, rows_in, pre_acts, acts, outputs = ([], [], [], [], [])
    incoming = None
    for tick in range(ticks):
        chunk = jnp.clip(tick - section_id, 0, chunks - 1)
        hidden = None
        if tick < chunks:
            hidden = chunk_of(tokens_in, chunk, 0).reshape(own_rows, width)
        if tick > 0:
            hidden = incoming if hidden is None else jnp.where(section_id == 0, hidden, incoming)
        widened, inv_rms = rms(hidden)
        gathered = gather((widened * inv_rms * gain_row).astype(jnp.bfloat16))
        pre = jnp.dot(gathered, w_in, preferred_element_type=jnp.float32).astype(jnp.bfloat16)
        gate, up = (pre[:, :inner].astype(jnp.float32), pre[:, inner:].astype(jnp.float32))
        act = (gate * jax.nn.sigmoid(gate) * up * spread_weights(chunk)).astype(jnp.bfloat16)
        mixed = jnp.dot(act, w_out, preferred_element_type=jnp.float32).astype(jnp.bfloat16)
        output = (widened + scatter(mixed).astype(jnp.float32)).astype(jnp.bfloat16)
        if tick < ticks - 1:
            incoming = from_behind(output, "section", 1)
        keep(hiddens, hidden, lambda c: tick - c)
        keep(rows_in, gathered, lambda c: tick - c)
        keep(pre_acts, pre, lambda c: tick - c)
        keep(acts, act, lambda c: tick - c)
        keep(outputs, output, lambda c: tick - c)
    grads_in, pre_grads, results = ([], [], [])
    for tick in range(ticks):
        chunk = jnp.clip(tick - (sections - 1 - section_id), 0, chunks - 1)
        active = {
            s: tick - (sections - 1 - s)
            for s in range(sections)
            if 0 <= tick - (sections - 1 - s) < chunks
        }
        grad_out = None
        if tick < chunks:
            grad_out = chunk_of(cotangent, chunk, 0).reshape(own_rows, width)
        if tick > 0:
            grad_out = (
                incoming
                if grad_out is None
                else jnp.where(section_id == sections - 1, grad_out, incoming)
            )
        gathered = gather(grad_out)
        pre = pick(section_id, {s: at(pre_acts, c, s) for s, c in active.items()})
        gate, up = (pre[:, :inner].astype(jnp.float32), pre[:, inner:].astype(jnp.float32))
        act_grad = lax.dot_general(
            gathered, w_out, (((1,), (1,)), ((), ())), preferred_element_type=jnp.float32
        )
        act_grad = act_grad * spread_weights(chunk)
        sig = jax.nn.sigmoid(gate)
        pre_grad = jnp.concatenate(
            [
                (act_grad * up * sig * (1.0 + gate * (1.0 - sig))).astype(jnp.bfloat16),
                (act_grad * gate * sig).astype(jnp.bfloat16),
            ],
            axis=1,
        )
        row_grad = lax.dot_general(
            pre_grad, w_in, (((1,), (1,)), ((), ())), preferred_element_type=jnp.float32
        ).astype(jnp.bfloat16)
        dnormed = scatter(row_grad).astype(jnp.float32)
        hidden = pick(section_id, {s: at(hiddens, c, s) for s, c in active.items()})
        widened, inv_rms = rms(hidden)
        unit = widened * inv_rms
        scaled = dnormed * gain_row
        result = (
            grad_out.astype(jnp.float32)
            + inv_rms * (scaled - unit * jnp.mean(scaled * unit, axis=-1, keepdims=True))
        ).astype(jnp.bfloat16)
        if tick < ticks - 1:
            incoming = from_behind(result, "section", -1)
        keep(grads_in, gathered, lambda c: sections - 1 - tick + c)
        keep(pre_grads, pre_grad, lambda c: sections - 1 - tick + c)
        keep(results, result, lambda c: sections - 1 - tick + c)

    def contract(left, right):
        return lax.dot_general(
            left, right, (((0,), (0,)), ((), ())), preferred_element_type=jnp.float32
        )

    def summed(pairs):
        total = contract(*pairs[0])
        for pair in pairs[1:]:
            total = total + contract(*pair)
        return total.astype(jnp.bfloat16)

    def split_columns(array, groups, part):
        size = array.shape[1] // groups
        piece = size // dp_count
        cuts = [
            lax.dynamic_slice_in_dim(array, g * size + part * piece, piece, 1)
            for g in range(groups)
        ]
        return cuts[0] if groups == 1 else jnp.concatenate(cuts, axis=1)

    def in_weight_part(part):

        def branch(section):
            back = sections - 1 - section
            return lambda: summed(
                [
                    (split_columns(at(rows_in, c, section), 1, part), at(pre_grads, c, back))
                    for c in range(chunks)
                ]
            )

        if compact:
            return branch(0)()
        return lax.switch(section_id, [branch(s) for s in range(sections)])

    def out_weight_part(part):

        def branch(section):
            back = sections - 1 - section
            return lambda: summed(
                [
                    (split_columns(at(acts, c, section), held, part), at(grads_in, c, back))
                    for c in range(chunks)
                ]
            )

        if compact:
            return branch(0)()
        return lax.switch(section_id, [branch(s) for s in range(sections)])

    dp_id = lax.axis_index("dp")

    def over_dp(part_fn):
        total = part_fn(dp_id).astype(jnp.float32)
        for distance in range(1, dp_count):
            ring = [(i, (i + distance) % dp_count) for i in range(dp_count)]
            other = part_fn((dp_id + distance) % dp_count)
            total = total + lax.ppermute(other, "dp", ring).astype(jnp.float32)
        return total.astype(jnp.bfloat16)

    out_grads = over_dp(out_weight_part)
    in_grads = over_dp(in_weight_part)
    grad_gate = jnp.stack(
        [in_grads[:, e * hidden_units : (e + 1) * hidden_units] for e in range(held)]
    )
    grad_up = jnp.stack(
        [
            in_grads[:, inner + e * hidden_units : inner + (e + 1) * hidden_units]
            for e in range(held)
        ]
    )
    grad_down = out_grads.reshape(held, hidden_units // dp_count, width)

    def in_order(per_tick, first_tick):
        kept = pick(
            section_id,
            {
                s: jnp.concatenate([at(per_tick, c, first_tick(s)) for c in range(chunks)], axis=0)
                for s in range(sections)
            },
        )
        return kept.reshape(1, micro_count, token_rows, width)

    layer_out = in_order(outputs, lambda s: s)
    input_grad = in_order(results, lambda s: sections - 1 - s)
    return (layer_out, input_grad, grad_gate[None], grad_up[None], grad_down[None])


def solution(mesh):
    placed = (
        P(None, ("expert", "dp"), None),
        P(None, ("expert", "dp"), None),
        P("section", None, ("expert", "dp"), None),
        P("section", None, ("expert", "dp"), None),
        P("section", None),
        P("section", "expert", None, None),
        P("section", "expert", None, None),
        P("section", "expert", None, None),
    )
    return jax.shard_map(
        on_device,
        mesh=mesh,
        in_specs=placed,
        out_specs=(
            P("section", None, ("expert", "dp"), None),
            P("section", None, ("expert", "dp"), None),
            P("section", "expert", "dp", None),
            P("section", "expert", "dp", None),
            P("section", "expert", "dp", None),
        ),
        check_vma=False,
    )
```

profile of v0, /device:TPU:0, one launch (start us, length us, event | category | flops | bytes accessed | tf_op | source)
XLA Modules:
  0.0 759.2 jit_solution(15389432934267854801)
XLA Ops:
  8.5 2.0 fusion.66
  12.2 7.3 all-to-all-start
  19.6 6.5 slice_bitcast_fusion.1
  28.0 1.4 broadcast_in_dim.36
  29.4 3.0 copy.35
  32.4 53.9 %all-gather.5.cloned.1.call-done = bf16[1024,2048]{1,0:T(8,128)(2,1)} async-done(((bf16[128,2048]{1,0:T(8,128)(2,1)}), bf16[1024,2048]{1,0:T(8,128)(2,1)}) %all-gather.5.cloned.1.call-update) | async-done | bytes 4194320 | tf_op jit(solution)/shard_map/all_gather | solution.py:66
  86.3 13.0 %convolution_convert_fusion.5 = bf16[1024,2048]{1,0:T(8,128)(2,1)S(1)} fusion(bf16[1024,2048]{1,0:T(8,128)(2,1)} %all-gather.5.cloned.1.call-done, bf16[2048,512]{1,0:T(8,128)(2,1)} %get-tuple-element.115, bf16[2048,512]{1,0:T(8,128)(2,1)S(1)} %get-tuple-element.114, bf16[2048,512]{1,0:T(8,128)(2,1)} %get-tuple-element.116, ...), kind=kOutput, calls=%fused_computation.84 | convolution fusion | flops 8625586176 | bytes 16777216 | tf_op jit(solution)/shard_map/dot_general | solution.py:102
  99.3 1.5 fusion.31
  101.4 1.6 copy-done.22
  103.0 6.2 convolution_convert_fusion.7
  109.3 87.0 %reduce-scatter.5.cloned.1.call-done = bf16[128,2048]{1,0:T(8,128)(2,1)} async-done(((bf16[1024,2048]{1,0:T(8,128)(2,1)}), bf16[128,2048]{1,0:T(8,128)(2,1)}) %reduce-scatter.5.cloned.1.call-update) | async-done | bytes 524304 | tf_op jit(solution)/shard_map/reduce_scatter | solution.py:69
  197.4 3.4 collective-permute-start
  200.8 10.8 %collective-permute-done = bf16[128,2048]{1,0:T(8,128)(2,1)S(1)} collective-permute-done((bf16[128,2048]{1,0:T(8,128)(2,1)S(1)}, bf16[128,2048]{1,0:T(8,128)(2,1)S(1)}, u32[]{:S(2)}, u32[]{:S(2)}) %collective-permute-start) | collective-permute-done | bytes 524320 | tf_op jit(solution)/shard_map/ppermute | solution.py:13
  213.6 73.3 %all-gather.7.cloned.1.call-done = bf16[1024,2048]{1,0:T(8,128)(2,1)} async-done(((bf16[128,2048]{1,0:T(8,128)(2,1)}), bf16[1024,2048]{1,0:T(8,128)(2,1)}) %all-gather.7.cloned.1.call-update) | async-done | bytes 4194320 | tf_op jit(solution)/shard_map/all_gather | solution.py:66
  286.9 14.3 %convolution_convert_fusion.4 = bf16[1024,2048]{1,0:T(8,128)(2,1)} fusion(bf16[1024,2048]{1,0:T(8,128)(2,1)} %all-gather.7.cloned.1.call-done, bf16[2048,512]{1,0:T(8,128)(2,1)} %get-tuple-element.115, bf16[2048,512]{1,0:T(8,128)(2,1)} %copy-done.18, bf16[2048,512]{1,0:T(8,128)(2,1)} %get-tuple-element.116, bf16[2048,512]{1,0:T(8,128)(2,1)} %get-tuple-element.117), kind=kOutput, calls=%fused_computation.83 | convolution fusion | flops 8625586176 | bytes 16777216 | tf_op jit(solution)/shard_map/dot_general | solution.py:102
  301.2 59.1 %all-gather.9.cloned.1.call-done = bf16[1024,2048]{1,0:T(8,128)(2,1)} async-done(((bf16[128,2048]{1,0:T(8,128)(2,1)}), bf16[1024,2048]{1,0:T(8,128)(2,1)}) %all-gather.9.cloned.1.call-update) | async-done | bytes 4194320 | tf_op jit(solution)/shard_map/all_gather | solution.py:66
  360.3 12.3 %fusion.39 = (bf16[1024,1024]{1,0:T(8,128)(2,1)S(1)}, bf16[1024,1024]{1,0:T(8,128)(2,1)S(1)}, bf16[1024,1024]{1,0:T(8,128)(2,1)}) fusion(bf16[1024,2048]{1,0:T(8,128)(2,1)} %convolution_convert_fusion.4, f32[1024,1024]{1,0:T(8,128)} %bitcast.77, bf16[1024,2048]{1,0:T(8,128)(2,1)} %all-gather.9.cloned.1.call-done, bf16[1024,2048]{1,0:T(8,128)(2,1)} %bitcast.96), kind=kOutput, calls=%fused_computation.65 | convolution fusion | flops 4315938816 | bytes 23068672 | tf_op jit(solution)/shard_map/dot_general | solution.py:134
  372.6 1.3 copy-done.10
  374.6 12.6 %convolution_convert_fusion.3 = bf16[1024,2048]{1,0:T(8,128)(2,1)} fusion(bf16[1024,1024]{1,0:T(8,128)(2,1)S(1)} %get-tuple-element.106, bf16[1024,1024]{1,0:T(8,128)(2,1)S(1)} %get-tuple-element.105, bf16[2048,512]{1,0:T(8,128)(2,1)} %get-tuple-element.115, bf16[2048,512]{1,0:T(8,128)(2,1)} %copy-done.18, bf16[2048,512]{1,0:T(8,128)(2,1)} %get-tuple-element.116, ...), kind=kOutput, calls=%fused_computation.82 | convolution fusion | flops 8633974784 | bytes 16777216 | tf_op jit(solution)/shard_map/dot_general | solution.py:146
  387.3 86.9 %reduce-scatter.9.cloned.1.call-done = bf16[128,2048]{1,0:T(8,128)(2,1)} async-done(((bf16[1024,2048]{1,0:T(8,128)(2,1)}), bf16[128,2048]{1,0:T(8,128)(2,1)}) %reduce-scatter.9.cloned.1.call-update) | async-done | bytes 524304 | tf_op jit(solution)/shard_map/reduce_scatter | solution.py:69
  474.2 1.4 fusion.56
  475.6 1.5 fusion.60
  477.9 1.3 collective-permute-start.1
  479.2 13.9 %collective-permute-done.1 = bf16[128,2048]{1,0:T(8,128)(2,1)S(1)} collective-permute-done((bf16[128,2048]{1,0:T(8,128)(2,1)S(1)}, bf16[128,2048]{1,0:T(8,128)(2,1)S(1)}, u32[]{:S(2)}, u32[]{:S(2)}) %collective-permute-start.1) | collective-permute-done | bytes 524320 | tf_op jit(solution)/shard_map/ppermute | solution.py:13
  494.4 9.4 %convolution_convert_fusion.6 = bf16[1024,2048]{1,0:T(8,128)(2,1)} fusion(bf16[1024,1024]{1,0:T(8,128)(2,1)} %get-tuple-element.111, bf16[1024,2048]{1,0:T(8,128)(2,1)} %bitcast.97), kind=kOutput, calls=%fused_computation.85 | convolution fusion | flops 4297064448 | bytes 10485760 | tf_op jit(solution)/shard_map/dot_general | solution.py:105
  503.8 62.4 %all-gather.11.cloned.1.call-done = bf16[1024,2048]{1,0:T(8,128)(2,1)} async-done(((bf16[128,2048]{1,0:T(8,128)(2,1)}), bf16[1024,2048]{1,0:T(8,128)(2,1)}) %all-gather.11.cloned.1.call-update) | async-done | bytes 4194320 | tf_op jit(solution)/shard_map/all_gather | solution.py:66
  566.1 11.9 %fusion.34 = (bf16[1024,1024]{1,0:T(8,128)(2,1)S(1)}, bf16[1024,1024]{1,0:T(8,128)(2,1)S(1)}) fusion(bf16[1024,2048]{1,0:T(8,128)(2,1)} %copy-done.4, f32[1024,1024]{1,0:T(8,128)} %bitcast.78, bf16[1024,2048]{1,0:T(8,128)(2,1)} %all-gather.11.cloned.1.call-done, bf16[1024,2048]{1,0:T(8,128)(2,1)} %bitcast.98), kind=kOutput, calls=%fused_computation.60 | convolution fusion | flops 4311744512 | bytes 20971520 | tf_op jit(solution)/shard_map/dot_general | solution.py:134
  578.0 1.3 copy-done.12
  580.0 12.7 %convolution_convert_fusion.2 = bf16[1024,2048]{1,0:T(8,128)(2,1)} fusion(bf16[1024,1024]{1,0:T(8,128)(2,1)S(1)} %get-tuple-element.104, bf16[1024,1024]{1,0:T(8,128)(2,1)S(1)} %get-tuple-element.103, bf16[2048,512]{1,0:T(8,128)(2,1)} %get-tuple-element.115, bf16[2048,512]{1,0:T(8,128)(2,1)} %copy-done.18, bf16[2048,512]{1,0:T(8,128)(2,1)} %get-tuple-element.116, ...), kind=kOutput, calls=%fused_computation.81 | convolution fusion | flops 8633974784 | bytes 16777216 | tf_op jit(solution)/shard_map/dot_general | solution.py:146
  592.8 5.1 pad_maximum_fusion.1
  597.9 2.4 pad_maximum_fusion.2
  600.3 9.6 %conditional.13 = (bf16[1024,2048]{1,0:T(8,128)(2,1)}) conditional(s32[]{:T(128)} %clamp.2, (s32[]{:T(128)}, bf16[1024,2048]{1,0:T(8,128)(2,1)}, bf16[1024,2048]{1,0:T(8,128)(2,1)}) %tuple.44, (s32[]{:T(128)}, bf16[1024,2048]{1,0:T(8,128)(2,1)}, bf16[1024,2048]{1,0:T(8,128)(2,1)}) %tuple.45), branch_computations={%region_11.12_spmd, %region_12.13_spmd} | conditional | flops 4294967296 | bytes 10485818
  600.5 9.4 %fusion.4 = bf16[1024,2048]{1,0:T(8,128)(2,1)} fusion(bf16[1024,2048]{1,0:T(8,128)(2,1)} %get-tuple-element.74, bf16[1024,2048]{1,0:T(8,128)(2,1)} %get-tuple-element.72, s32[]{:T(128)S(6)} %select_n.46), kind=kOutput, calls=%fused_computation.6 | convolution fusion | flops 4294967296 | bytes 10485764 | tf_op jit(solution)/shard_map/cond/branch_0_fun/dot_general | solution.py:165
  609.9 6.3 conditional.15
  610.0 6.0 fusion.20
  616.8 39.9 %reduce-scatter.7.cloned.1.call-done = bf16[128,2048]{1,0:T(8,128)(2,1)} async-done(((bf16[1024,2048]{1,0:T(8,128)(2,1)}), bf16[128,2048]{1,0:T(8,128)(2,1)}) %reduce-scatter.7.cloned.1.call-update) | async-done | bytes 524304 | tf_op jit(solution)/shard_map/reduce_scatter | solution.py:69
  656.7 2.1 fusion.75
  658.7 10.7 %conditional.12 = (f32[1024,2048]{1,0:T(8,128)}) conditional(s32[]{:T(128)} %clamp.2, (s32[]{:T(128)}, bf16[1024,2048]{1,0:T(8,128)(2,1)}, bf16[1024,2048]{1,0:T(8,128)(2,1)}) %tuple.42, (s32[]{:T(128)}, bf16[1024,2048]{1,0:T(8,128)(2,1)}, bf16[1024,2048]{1,0:T(8,128)(2,1)}) %tuple.43), branch_computations={%region_9.10_spmd, %region_10.11_spmd} | conditional | flops 4299161600 | bytes 14680122 | solution.py:197
  658.7 10.7 %convert_convert_fusion = f32[1024,2048]{1,0:T(8,128)} fusion(bf16[1024,2048]{1,0:T(8,128)(2,1)} %get-tuple-element.68, bf16[1024,2048]{1,0:T(8,128)(2,1)} %get-tuple-element.66, s32[]{:T(128)S(6)} %select_n.44), kind=kOutput, calls=%fused_computation | convolution fusion | flops 4299161600 | bytes 14680068 | tf_op jit(solution)/shard_map/cond/branch_0_fun/dot_general | solution.py:165
  669.4 7.0 conditional.14
  669.8 6.6 fusion.10
  676.4 5.1 add_convert_fusion.1
  682.6 3.8 add_convert_fusion
  686.8 1.5 maximum_bitcast_fusion
  688.3 1.5 maximum_bitcast_fusion.1
  689.8 58.4 %reduce-scatter.11.cloned.1.call-done = bf16[128,2048]{1,0:T(8,128)(2,1)} async-done(((bf16[1024,2048]{1,0:T(8,128)(2,1)}), bf16[128,2048]{1,0:T(8,128)(2,1)}) %reduce-scatter.11.cloned.1.call-update) | async-done | bytes 524304 | tf_op jit(solution)/shard_map/reduce_scatter | solution.py:69
  748.2 1.4 fusion.67
  749.6 2.3 fusion.74
  (82 shorter events, 14.7 us)
Async XLA Ops:
  7.2 79.1 %all-gather.5.cloned.1.call-start = ((), (), s32[]{:S(2)}) async-start(), calls=%async_computation.5 | async-start | bytes 4718592 | tf_op jit(solution)/shard_map/all_gather | solution.py:66
  8.5 2.1 copy-start.20
  12.2 13.9 %all-to-all-start = ((f32[8,1,256]{2,1,0:T(1,128)}), f32[8,1,256]{2,1,0:T(1,128)S(1)}, u32[]{:S(2)}, u32[]{:S(2)}) async-start(f32[8,1,256]{2,1,0:T(1,128)} %reshape.77), calls=%async_computation | async-start | bytes 16384 | tf_op jit(solution)/shard_map/all_to_all | solution.py:29
  19.5 176.7 %reduce-scatter.5.cloned.1.call-start = ((), (), s32[]{:S(2)}) async-start(), calls=%async_computation.6 | async-start | bytes 4718592 | tf_op jit(solution)/shard_map/reduce_scatter | solution.py:69
  26.1 60.2 %copy-start.18 = (bf16[2048,512]{1,0:T(8,128)(2,1)}, bf16[2048,512]{1,0:T(8,128)(2,1)S(1)}, u32[]{:S(2)}) copy-start(bf16[2048,512]{1,0:T(8,128)(2,1)S(1)} %get-tuple-element.114) | copy-start | bytes 6291460
  86.3 13.1 %copy-start = (f32[128,8,2,512]{3,1,2,0:T(8,128)S(1)}, f32[128,8,2,512]{3,1,2,0:T(8,128)}, u32[]{:S(2)}) copy-start(f32[128,8,2,512]{3,1,2,0:T(8,128)} %copy.35) | copy-start | bytes 12582916
  99.3 2.1 copy-start.4
  99.3 3.7 copy-start.22
  109.2 87.0 %copy-start.1 = (bf16[8,16,2048]{2,1,0:T(8,128)(2,1)S(1)}, bf16[8,16,2048]{2,1,0:T(8,128)(2,1)}, u32[]{:S(2)}) copy-start(bf16[8,16,2048]{2,1,0:T(8,128)(2,1)} %param.16) | copy-start | bytes 1572868
  109.2 102.6 %copy-start.19 = (f32[1,2048]{1,0:T(1,128)S(1)}, f32[1,2048]{1,0:T(1,128)}, u32[]{:S(2)}) copy-start(f32[1,2048]{1,0:T(1,128)} %param.20) | copy-start | bytes 24580
  109.2 177.7 %all-gather.7.cloned.1.call-start = ((), (), s32[]{:S(2)}) async-start(), calls=%async_computation.7 | async-start | bytes 4718592 | tf_op jit(solution)/shard_map/all_gather | solution.py:66
  197.4 14.2 %copy-start.5 = (bf16[128,2048]{1,0:T(8,128)(2,1)}, bf16[128,2048]{1,0:T(8,128)(2,1)S(1)}, u32[]{:S(2)}) copy-start(bf16[128,2048]{1,0:T(8,128)(2,1)S(1)} %fusion.73) | copy-start | bytes 1572868
  197.4 14.2 %collective-permute-start = (bf16[128,2048]{1,0:T(8,128)(2,1)S(1)}, bf16[128,2048]{1,0:T(8,128)(2,1)S(1)}, u32[]{:S(2)}, u32[]{:S(2)}) collective-permute-start(bf16[128,2048]{1,0:T(8,128)(2,1)S(1)} %fusion.73), channel_id=1, source_target_pairs={{0,16},{1,17},{2,18},{3,19},{4,20},{5,21},{6,22},{7,23},{8,24},{9,... | collective-permute-start | bytes 1572872 | tf_op jit(solution)/shard_map/ppermute | solution.py:13
  212.8 147.5 %all-gather.9.cloned.1.call-start = ((), (), s32[]{:S(2)}) async-start(), calls=%async_computation.9 | async-start | bytes 4718592 | tf_op jit(solution)/shard_map/all_gather | solution.py:66
  213.4 260.8 %reduce-scatter.9.cloned.1.call-start = ((), (), s32[]{:S(2)}) async-start(), calls=%async_computation.10 | async-start | bytes 4718592 | tf_op jit(solution)/shard_map/reduce_scatter | solution.py:69
  372.6 1.3 copy-start.10
  372.6 2.0 copy-start.11
  387.2 88.4 %copy-start.7 = (bf16[8,16,2048]{2,1,0:T(8,128)(2,1)S(1)}, bf16[8,16,2048]{2,1,0:T(8,128)(2,1)}, u32[]{:S(2)}) copy-start(bf16[8,16,2048]{2,1,0:T(8,128)(2,1)} %param.17) | copy-start | bytes 1572868
  387.2 178.9 %all-gather.11.cloned.1.call-start = ((), (), s32[]{:S(2)}) async-start(), calls=%async_computation.11 | async-start | bytes 4718592 | tf_op jit(solution)/shard_map/all_gather | solution.py:66
  477.0 0.8 copy-start.16
  477.9 15.2 %collective-permute-start.1 = (bf16[128,2048]{1,0:T(8,128)(2,1)S(1)}, bf16[128,2048]{1,0:T(8,128)(2,1)S(1)}, u32[]{:S(2)}, u32[]{:S(2)}) collective-permute-start(bf16[128,2048]{1,0:T(8,128)(2,1)S(1)} %fusion.60), channel_id=1, source_target_pairs={{16,0},{17,1},{18,2},{19,3},{20,4},{21,5},{22,6},{23,7},{24,8},{25... | collective-permute-start | bytes 1572872 | tf_op jit(solution)/shard_map/ppermute | solution.py:13
  493.0 0.8 copy-start.8
  493.9 162.8 %reduce-scatter.7.cloned.1.call-start = ((), (), s32[]{:S(2)}) async-start(), calls=%async_computation.8 | async-start | bytes 4718592 | tf_op jit(solution)/shard_map/reduce_scatter | solution.py:69
  503.7 244.5 %reduce-scatter.11.cloned.1.call-start = ((), (), s32[]{:S(2)}) async-start(), calls=%async_computation.12 | async-start | bytes 4718592 | tf_op jit(solution)/shard_map/reduce_scatter | solution.py:69
  578.0 1.3 copy-start.12
  578.0 2.0 copy-start.14
  592.7 5.1 copy-start.13
  592.8 5.1 copy-start.15
  609.9 71.7 %collective-permute-start.2 = (bf16[1024,2048]{1,0:T(8,128)(2,1)}, bf16[1024,2048]{1,0:T(8,128)(2,1)}, u32[]{:S(2)}, u32[]{:S(2)}) collective-permute-start(bf16[1024,2048]{1,0:T(8,128)(2,1)} %get-tuple-element.119), channel_id=1, source_target_pairs={{0,1},{1,0},{2,3},{3,2},{4,5},{5,4},{6,7},{7,6},{8,9},{9,8},{10,11... | collective-permute-start | bytes 12582920 | tf_op jit(solution)/shard_map/ppermute | solution.py:221
  609.9 46.8 %copy-start.6 = (bf16[128,2048]{1,0:T(8,128)(2,1)S(1)}, bf16[128,2048]{1,0:T(8,128)(2,1)}, u32[]{:S(2)}) copy-start(bf16[128,2048]{1,0:T(8,128)(2,1)} %copy-done.5) | copy-start | bytes 1572868
  616.2 60.2 %collective-permute-start.3 = (bf16[512,2048]{1,0:T(8,128)(2,1)}, bf16[512,2048]{1,0:T(8,128)(2,1)}, u32[]{:S(2)}, u32[]{:S(2)}) collective-permute-start(bf16[512,2048]{1,0:T(8,128)(2,1)} %get-tuple-element.121), channel_id=1, source_target_pairs={{0,1},{1,0},{2,3},{3,2},{4,5},{5,4},{6,7},{7,6},{8,9},{9,8},{10,11... | collective-permute-start | bytes 6291464 | tf_op jit(solution)/shard_map/ppermute | solution.py:221
  676.4 6.2 copy-start.3
  686.8 61.5 %copy-start.2 = (bf16[8,16,2048]{2,1,0:T(8,128)(2,1)S(1)}, bf16[8,16,2048]{2,1,0:T(8,128)(2,1)}, u32[]{:S(2)}) copy-start(bf16[8,16,2048]{2,1,0:T(8,128)(2,1)} %param.16) | copy-start | bytes 1572868
  686.8 61.5 %copy-start.21 = (f32[128]{0:T(128)S(1)}, f32[128]{0:T(128)}, u32[]{:S(2)}) copy-start(f32[128]{0:T(128)} %copy-done.20) | copy-start | bytes 1540
  686.8 62.8 %copy-start.9 = (bf16[128,2048]{1,0:T(8,128)(2,1)S(1)}, bf16[128,2048]{1,0:T(8,128)(2,1)}, u32[]{:S(2)}) copy-start(bf16[128,2048]{1,0:T(8,128)(2,1)} %copy-done.8) | copy-start | bytes 1572868
  686.8 62.8 %copy-start.17 = (bf16[128,2048]{1,0:T(8,128)(2,1)S(1)}, bf16[128,2048]{1,0:T(8,128)(2,1)}, u32[]{:S(2)}) copy-start(bf16[128,2048]{1,0:T(8,128)(2,1)} %copy-done.16) | copy-start | bytes 1572868
Sparse Core Ops, SparseCore 0:
  10.7 75.4 all-gather.4
  109.3 86.8 reduce-scatter.4
  212.9 73.9 all-gather.6
  288.9 71.3 all-gather.8
  387.3 86.8 reduce-scatter.8
  494.0 72.0 all-gather.10
  569.8 86.8 reduce-scatter.6
  660.3 87.9 reduce-scatter.10
where the time goes:
time: 768 us; the launch traced here: 759 us
  waiting for transfers between devices  546 us (71%)
  matrix products  125 us (16%)
  other arithmetic  36.8 us (5%)
  local copies, waits for them, and re-layouts  22.3 us (3%)
  between operations  14.9 us (2%)
  starting transfers between devices  13.5 us (2%)
    reduce_scatter x4, waiting for transfers between devices, scatter(): return lax.psum_scatter(rows, 'expert', scatter_dimension=0, tiled=True)  272 us
    all_gather x4, waiting for transfers between devices, gather(): return lax.all_gather(rows, 'expert', axis=0, tiled=True)  249 us
    dot_general x4, matrix products, contract(): lax.dot_general(left, right, (((0,), (0,)), ((), ())), preferred_element_...  32.7 us
    dot_general x2, matrix products, on_device(): jnp.dot(gathered, w_in, preferred_element_type=jnp.float32)  27.3 us
    dot_general x2, matrix products, on_device(): lax.dot_general(pre_grad, w_in, (((1,), (1,)), ((), ())), preferred_eleme...  25.3 us
    ppermute x2, waiting for transfers between devices, from_behind(): return lax.ppermute(block, axis, route)  24.6 us
    dot_general x2, matrix products, on_device(): lax.dot_general(gathered, w_out, (((1,), (1,)), ((), ())), preferred_elem...  24.2 us
    dot_general x2, matrix products, on_device(): jnp.dot(act, w_out, preferred_element_type=jnp.float32).astype(jnp.bfloat16)  15.5 us
  transfers between devices with their start and end apart: 13, of which 11 were waited for; matrix products, arithmetic and copies ran while one was open for 15% of the time, Pallas kernels for 0%

commit v1 on v0

--- a/solution.py
+++ b/solution.py
@@ -5,6 +5,22 @@
 
 epsilon = 1e-06
 ROW_LIMIT = 1024
+
+
+def _spread_field(x_part, across, out_dim):
+    total_devices = lax.axis_size(across)
+    so_far_all = tuple(((k, (k + 1) % total_devices) for k in range(total_devices)))
+    pile = tuple(((k, (k - 1) % total_devices) for k in range(total_devices)))
+    arr_next, w1 = ([x_part], [x_part])
+    for _ in range(total_devices // 2):
+        arr_next.append(lax.ppermute(arr_next[-1], axis_name=across, perm=so_far_all))
+    for _ in [*range((total_devices - 1) // 2)]:
+        w1.append(lax.ppermute(w1[-1], across, pile))
+    out_arr = jnp.concatenate([*arr_next[::-1], *w1[1:]], axis=out_dim)
+    main = jnp.roll(
+        out_arr, (lax.axis_index(across) - total_devices // 2) * x_part.shape[out_dim], axis=out_dim
+    )
+    return main
 
 
 def from_behind(block, axis, distance):
@@ -63,7 +79,7 @@
         return jnp.repeat(rows, hidden_units, axis=1)
 
     def gather(rows):
-        return lax.all_gather(rows, "expert", axis=0, tiled=True)
+        return _spread_field(rows, across="expert", out_dim=0)
 
     def scatter(rows):
         return lax.psum_scatter(rows, "expert", scatter_dimension=0, tiled=True)

time: 768 us -> 797 us (1.038)
  starting transfers between devices: 13.5 us -> 93 us
  waiting for transfers between devices: 546 us -> 481 us
  other arithmetic: 36.8 us -> 53.2 us
    all_gather x4 -> x0, waiting for transfers between devices: 249 us -> none  [gather(): return lax.all_gather(rows, 'expert', axis=0, tiled=True)]
    ppermute x0 -> x28, waiting for transfers between devices: none -> 235 us  [the longest x16 210 us: _spread_field(): lax.ppermute(arr_next[-1], axis_name=across, perm=so_far_all)]
    ppermute x0 -> x28, starting transfers between devices: none -> 82.7 us  [the longest x12 54.1 us: _spread_field(): w1.append(lax.ppermute(w1[-1], across, pile))]
    reduce_scatter x4, waiting for transfers between devices: 272 us -> 221 us  [scatter(): return lax.psum_scatter(rows, 'expert', scatter_dimension=0, tiled=True)]
    concatenate x0 -> x3, other arithmetic: none -> 18.6 us  [_spread_field(): jnp.roll(out_arr, (lax.axis_index(across) - total_devices // 2) * x_part....]
    unnamed x49 -> x100, local copies, waits for them, and re-layouts: 12.6 us -> 17.8 us
  transfers between devices with their start and end apart: 13 -> 37, of which waited for: 11 -> 24; matrix products, arithmetic and copies ran while one was open for 15% -> 14% of each run, Pallas kernels for 0% -> 0%
where the time goes in v1:
time: 797 us; the launch traced here: 792 us
  waiting for transfers between devices  481 us (60%)
  matrix products  123 us (15%)
  starting transfers between devices  93 us (12%)
  other arithmetic  53.2 us (7%)
  local copies, waits for them, and re-layouts  27 us (3%)
  between operations  14.8 us (2%)
    reduce_scatter x4, waiting for transfers between devices, scatter(): return lax.psum_scatter(rows, 'expert', scatter_dimension=0, tiled=True)  221 us
    ppermute x16, waiting for transfers between devices, _spread_field(): lax.ppermute(arr_next[-1], axis_name=across, perm=so_far_all)  210 us
    ppermute x12, starting transfers between devices, _spread_field(): w1.append(lax.ppermute(w1[-1], across, pile))  54.1 us
    dot_general x4, matrix products, contract(): lax.dot_general(left, right, (((0,), (0,)), ((), ())), preferred_element_...  32.8 us
    ppermute x16, starting transfers between devices, _spread_field(): lax.ppermute(arr_next[-1], axis_name=across, perm=so_far_all)  28.6 us
    dot_general x2, matrix products, on_device(): jnp.dot(gathered, w_in, preferred_element_type=jnp.float32)  27.6 us
    dot_general x2, matrix products, on_device(): lax.dot_general(pre_grad, w_in, (((1,), (1,)), ((), ())), preferred_eleme...  27 us
    ppermute x2, waiting for transfers between devices, from_behind(): return lax.ppermute(block, axis, route)  24.6 us
  transfers between devices with their start and end apart: 37, of which 24 were waited for; matrix products, arithmetic and copies ran while one was open for 14% of the time, Pallas kernels for 0%

profile of v1, /device:TPU:0, one launch (start us, length us, event | category | flops | bytes accessed | tf_op | source)
XLA Modules:
  0.0 792.5 jit_solution(1853880099463762897)
XLA Ops:
  14.4 11.9 %collective-permute-done.15 = bf16[128,2048]{1,0:T(8,128)(2,1)S(1)} collective-permute-done((bf16[128,2048]{1,0:T(8,128)(2,1)}, bf16[128,2048]{1,0:T(8,128)(2,1)S(1)}, u32[]{:S(2)}, u32[]{:S(2)}) %collective-permute-start.15) | collective-permute-done | bytes 524320 | tf_op jit(solution)/shard_map/ppermute | solution.py:16
  26.2 4.7 collective-permute-start.19
  31.0 25.5 %collective-permute-done = bf16[128,2048]{1,0:T(8,128)(2,1)S(1)} collective-permute-done((bf16[128,2048]{1,0:T(8,128)(2,1)S(1)}, bf16[128,2048]{1,0:T(8,128)(2,1)S(1)}, u32[]{:S(2)}, u32[]{:S(2)}) %collective-permute-start) | collective-permute-done | bytes 524320 | tf_op jit(solution)/shard_map/ppermute | solution.py:16
  58.9 8.8 %collective-permute-done.16 = bf16[128,2048]{1,0:T(8,128)(2,1)S(1)} collective-permute-done((bf16[128,2048]{1,0:T(8,128)(2,1)S(1)}, bf16[128,2048]{1,0:T(8,128)(2,1)S(1)}, u32[]{:S(2)}, u32[]{:S(2)}) %collective-permute-start.16) | collective-permute-done | bytes 524320 | tf_op jit(solution)/shard_map/ppermute | solution.py:16
  71.8 4.9 all-to-all-start
  76.7 4.7 collective-permute-start.20
  81.4 11.5 %collective-permute-done.4 = bf16[128,2048]{1,0:T(8,128)(2,1)S(1)} collective-permute-done((bf16[128,2048]{1,0:T(8,128)(2,1)S(1)}, bf16[128,2048]{1,0:T(8,128)(2,1)S(1)}, u32[]{:S(2)}, u32[]{:S(2)}) %collective-permute-start.4) | collective-permute-done | bytes 524320 | tf_op jit(solution)/shard_map/ppermute | solution.py:18
  95.0 17.7 %collective-permute-done.17 = bf16[128,2048]{1,0:T(8,128)(2,1)} collective-permute-done((bf16[128,2048]{1,0:T(8,128)(2,1)S(1)}, bf16[128,2048]{1,0:T(8,128)(2,1)}, u32[]{:S(2)}, u32[]{:S(2)}) %collective-permute-start.17) | collective-permute-done | bytes 524320 | tf_op jit(solution)/shard_map/ppermute | solution.py:16
  115.2 6.0 slice_bitcast_fusion.1
  128.5 9.5 %collective-permute-done.5 = bf16[128,2048]{1,0:T(8,128)(2,1)} collective-permute-done((bf16[128,2048]{1,0:T(8,128)(2,1)S(1)}, bf16[128,2048]{1,0:T(8,128)(2,1)}, u32[]{:S(2)}, u32[]{:S(2)}) %collective-permute-start.5) | collective-permute-done | bytes 524320 | tf_op jit(solution)/shard_map/ppermute | solution.py:18
  140.3 17.4 %collective-permute-done.18 = bf16[128,2048]{1,0:T(8,128)(2,1)} collective-permute-done((bf16[128,2048]{1,0:T(8,128)(2,1)}, bf16[128,2048]{1,0:T(8,128)(2,1)}, u32[]{:S(2)}, u32[]{:S(2)}) %collective-permute-start.18) | collective-permute-done | bytes 524320 | tf_op jit(solution)/shard_map/ppermute | solution.py:16
  160.1 7.8 collective-permute-done.3
  172.5 8.3 %fusion.53 = (bf16[1024,2048]{1,0:T(8,128)(2,1)}, bf16[1024,2048]{1,0:T(8,128)(2,1)S(1)}) fusion(s32[]{:T(128)S(6)} %select_n.82, bf16[1024,2048]{1,0:T(8,128)(2,1)S(1)} %constant_dynamic-update-slice_fusion.16, bf16[1024,2048]{1,0:T(8,128)(2,1)S(1)} %constant_dynamic-update-slice_fusion), kind=kLoop, calls=%fused_computation.87 | loop fusion | flops 16777216 | bytes 16777220 | tf_op jit(solution)/shard_map/jit(_roll_dynamic)/concatenate | solution.py:20
  180.8 13.1 %convolution_convert_fusion.5 = bf16[1024,2048]{1,0:T(8,128)(2,1)S(1)} fusion(bf16[1024,2048]{1,0:T(8,128)(2,1)S(1)} %get-tuple-element.118, bf16[2048,512]{1,0:T(8,128)(2,1)} %get-tuple-element.116, bf16[2048,512]{1,0:T(8,128)(2,1)} %get-tuple-element.115, bf16[2048,512]{1,0:T(8,128)(2,1)} %get-tuple-element.119, bf16[2048,512]{1,0:T(8,128)(2,1)} %get-tuple-element.120), kind=kOutput, calls=%fused_computation.96 | convolution fusion | flops 8625586176 | bytes 16777216 | tf_op jit(solution)/shard_map/dot_general | solution.py:118
  198.5 6.1 convolution_convert_fusion.7
  204.7 90.5 %reduce-scatter.5.cloned.1.call-done = bf16[128,2048]{1,0:T(8,128)(2,1)} async-done(((bf16[1024,2048]{1,0:T(8,128)(2,1)}), bf16[128,2048]{1,0:T(8,128)(2,1)}) %reduce-scatter.5.cloned.1.call-update) | async-done | bytes 524304 | tf_op jit(solution)/shard_map/reduce_scatter | solution.py:85
  299.8 10.8 %collective-permute-done.7 = bf16[128,2048]{1,0:T(8,128)(2,1)S(1)} collective-permute-done((bf16[128,2048]{1,0:T(8,128)(2,1)S(1)}, bf16[128,2048]{1,0:T(8,128)(2,1)S(1)}, u32[]{:S(2)}, u32[]{:S(2)}) %collective-permute-start.7) | collective-permute-done | bytes 524320 | tf_op jit(solution)/shard_map/ppermute | solution.py:29
  312.5 13.7 %collective-permute-done.8 = bf16[128,2048]{1,0:T(8,128)(2,1)S(1)} collective-permute-done((bf16[128,2048]{1,0:T(8,128)(2,1)S(1)}, bf16[128,2048]{1,0:T(8,128)(2,1)S(1)}, u32[]{:S(2)}, u32[]{:S(2)}) %collective-permute-start.8) | collective-permute-done | bytes 524320 | tf_op jit(solution)/shard_map/ppermute | solution.py:16
  326.1 4.7 collective-permute-start.12
  330.9 15.9 %collective-permute-done.9 = bf16[128,2048]{1,0:T(8,128)(2,1)S(1)} collective-permute-done((bf16[128,2048]{1,0:T(8,128)(2,1)S(1)}, bf16[128,2048]{1,0:T(8,128)(2,1)S(1)}, u32[]{:S(2)}, u32[]{:S(2)}) %collective-permute-start.9) | collective-permute-done | bytes 524320 | tf_op jit(solution)/shard_map/ppermute | solution.py:16
  349.8 12.4 %collective-permute-start.13 = (bf16[128,2048]{1,0:T(8,128)(2,1)S(1)}, bf16[128,2048]{1,0:T(8,128)(2,1)S(1)}, u32[]{:S(2)}, u32[]{:S(2)}) collective-permute-start(bf16[128,2048]{1,0:T(8,128)(2,1)S(1)} %collective-permute-done.12), channel_id=1, source_target_pairs={{0,14},{2,0},{4,2},{6,4},{8,6},{10,8},{12,10},{14,12},{1,15},{3,1}... | collective-permute-start | bytes 1572872 | tf_op jit(solution)/shard_map/ppermute | solution.py:18
  362.1 8.6 %collective-permute-done.10 = bf16[128,2048]{1,0:T(8,128)(2,1)S(1)} collective-permute-done((bf16[128,2048]{1,0:T(8,128)(2,1)S(1)}, bf16[128,2048]{1,0:T(8,128)(2,1)S(1)}, u32[]{:S(2)}, u32[]{:S(2)}) %collective-permute-start.10) | collective-permute-done | bytes 524320 | tf_op jit(solution)/shard_map/ppermute | solution.py:16
  373.5 13.7 %collective-permute-start.14 = (bf16[128,2048]{1,0:T(8,128)(2,1)S(1)}, bf16[128,2048]{1,0:T(8,128)(2,1)S(1)}, u32[]{:S(2)}, u32[]{:S(2)}) collective-permute-start(bf16[128,2048]{1,0:T(8,128)(2,1)S(1)} %collective-permute-done.13), channel_id=1, source_target_pairs={{0,14},{2,0},{4,2},{6,4},{8,6},{10,8},{12,10},{14,12},{1,15},{3,1}... | collective-permute-start | bytes 1572872 | tf_op jit(solution)/shard_map/ppermute | solution.py:18
  387.2 7.3 collective-permute-done.11
  397.8 5.7 fusion.54
  403.5 14.4 %convolution_convert_fusion.4 = bf16[1024,2048]{1,0:T(8,128)(2,1)} fusion(bf16[1024,2048]{1,0:T(8,128)(2,1)} %fusion.54, bf16[2048,512]{1,0:T(8,128)(2,1)} %get-tuple-element.116, bf16[2048,512]{1,0:T(8,128)(2,1)S(1)} %copy-done.27, bf16[2048,512]{1,0:T(8,128)(2,1)} %get-tuple-element.119, bf16[2048,512]{1,0:T(8,128)(2,1)} %get-tuple-element.120), kind=kOutput, calls=%fused_computation.95 | convolution fusion | flops 8625586176 | bytes 16777216 | tf_op jit(solution)/shard_map/dot_general | solution.py:118
  417.9 10.9 %fusion.39 = (bf16[1024,1024]{1,0:T(8,128)(2,1)}, bf16[1024,1024]{1,0:T(8,128)(2,1)}, bf16[1024,1024]{1,0:T(8,128)(2,1)S(1)}) fusion(bf16[1024,2048]{1,0:T(8,128)(2,1)} %convolution_convert_fusion.4, f32[1024,1024]{1,0:T(8,128)S(1)} %bitcast.78, bf16[1024,2048]{1,0:T(8,128)(2,1)S(1)} %copy-done.8, bf16[1024,2048]{1,0:T(8,128)(2,1)} %bitcast.99), kind=kOutput, calls=%fused_computation.73 | convolution fusion | flops 4315938816 | bytes 23068672 | tf_op jit(solution)/shard_map/dot_general | solution.py:150
  428.9 14.7 %convolution_convert_fusion.3 = bf16[1024,2048]{1,0:T(8,128)(2,1)} fusion(bf16[1024,1024]{1,0:T(8,128)(2,1)} %get-tuple-element.107, bf16[1024,1024]{1,0:T(8,128)(2,1)} %get-tuple-element.106, bf16[2048,512]{1,0:T(8,128)(2,1)} %get-tuple-element.116, bf16[2048,512]{1,0:T(8,128)(2,1)} %get-tuple-element.115, bf16[2048,512]{1,0:T(8,128)(2,1)} %get-tuple-element.119, ...), kind=kOutput, calls=%fused_computation.94 | convolution fusion | flops 8633974784 | bytes 16777216 | tf_op jit(solution)/shard_map/dot_general | solution.py:162
  443.7 91.3 %reduce-scatter.9.cloned.1.call-done = bf16[128,2048]{1,0:T(8,128)(2,1)} async-done(((bf16[1024,2048]{1,0:T(8,128)(2,1)}), bf16[128,2048]{1,0:T(8,128)(2,1)}) %reduce-scatter.9.cloned.1.call-update) | async-done | bytes 524304 | tf_op jit(solution)/shard_map/reduce_scatter | solution.py:85
  539.1 13.9 %collective-permute-done.22 = bf16[128,2048]{1,0:T(8,128)(2,1)S(1)} collective-permute-done((bf16[128,2048]{1,0:T(8,128)(2,1)S(1)}, bf16[128,2048]{1,0:T(8,128)(2,1)S(1)}, u32[]{:S(2)}, u32[]{:S(2)}) %collective-permute-start.22) | collective-permute-done | bytes 524320 | tf_op jit(solution)/shard_map/ppermute | solution.py:29
  554.5 8.3 %convolution_convert_fusion.6 = bf16[1024,2048]{1,0:T(8,128)(2,1)} fusion(bf16[1024,1024]{1,0:T(8,128)(2,1)S(1)} %get-tuple-element.112, bf16[1024,2048]{1,0:T(8,128)(2,1)} %bitcast.100), kind=kOutput, calls=%fused_computation.97 | convolution fusion | flops 4297064448 | bytes 10485760 | tf_op jit(solution)/shard_map/dot_general | solution.py:121
  562.8 5.4 collective-permute-done.23
  568.2 4.7 collective-permute-start.27
  572.9 21.8 %collective-permute-done.24 = bf16[128,2048]{1,0:T(8,128)(2,1)S(1)} collective-permute-done((bf16[128,2048]{1,0:T(8,128)(2,1)}, bf16[128,2048]{1,0:T(8,128)(2,1)S(1)}, u32[]{:S(2)}, u32[]{:S(2)}) %collective-permute-start.24) | collective-permute-done | bytes 524320 | tf_op jit(solution)/shard_map/ppermute | solution.py:16
  599.5 24.4 %collective-permute-done.25 = bf16[128,2048]{1,0:T(8,128)(2,1)S(1)} collective-permute-done((bf16[128,2048]{1,0:T(8,128)(2,1)S(1)}, bf16[128,2048]{1,0:T(8,128)(2,1)S(1)}, u32[]{:S(2)}, u32[]{:S(2)}) %collective-permute-start.25) | collective-permute-done | bytes 524320 | tf_op jit(solution)/shard_map/ppermute | solution.py:16
  628.8 24.6 %collective-permute-done.26 = bf16[128,2048]{1,0:T(8,128)(2,1)S(1)} collective-permute-done((bf16[128,2048]{1,0:T(8,128)(2,1)S(1)}, bf16[128,2048]{1,0:T(8,128)(2,1)S(1)}, u32[]{:S(2)}, u32[]{:S(2)}) %collective-permute-start.26) | collective-permute-done | bytes 524320 | tf_op jit(solution)/shard_map/ppermute | solution.py:16
  659.7 10.1 %fusion.34 = (bf16[1024,1024]{1,0:T(8,128)(2,1)S(1)}, bf16[1024,1024]{1,0:T(8,128)(2,1)S(1)}) fusion(bf16[1024,2048]{1,0:T(8,128)(2,1)S(1)} %copy-done.12, f32[1024,1024]{1,0:T(8,128)S(1)} %bitcast.79, bf16[1024,2048]{1,0:T(8,128)(2,1)S(1)} %fusion.52, bf16[1024,2048]{1,0:T(8,128)(2,1)} %bitcast.101), kind=kOutput, calls=%fused_computation.68 | convolution fusion | flops 4311744512 | bytes 20971520 | tf_op jit(solution)/shard_map/dot_general | solution.py:150
  671.9 12.3 %convolution_convert_fusion.2 = bf16[1024,2048]{1,0:T(8,128)(2,1)} fusion(bf16[1024,1024]{1,0:T(8,128)(2,1)S(1)} %get-tuple-element.105, bf16[1024,1024]{1,0:T(8,128)(2,1)S(1)} %get-tuple-element.104, bf16[2048,512]{1,0:T(8,128)(2,1)} %get-tuple-element.116, bf16[2048,512]{1,0:T(8,128)(2,1)S(1)} %copy-done.28, bf16[2048,512]{1,0:T(8,128)(2,1)} %get-tuple-element.119, ...), kind=kOutput, calls=%fused_computation.93 | convolution fusion | flops 8633974784 | bytes 16777216 | tf_op jit(solution)/shard_map/dot_general | solution.py:162
  692.5 10.0 %conditional.13 = (bf16[1024,2048]{1,0:T(8,128)(2,1)}) conditional(s32[]{:T(128)} %clamp.2, (s32[]{:T(128)}, bf16[1024,2048]{1,0:T(8,128)(2,1)}, bf16[1024,2048]{1,0:T(8,128)(2,1)}) %tuple.85, (s32[]{:T(128)}, bf16[1024,2048]{1,0:T(8,128)(2,1)}, bf16[1024,2048]{1,0:T(8,128)(2,1)}) %tuple.46), branch_computations={%region_11.13_spmd, %region_12.14_spmd} | conditional | flops 4294967296 | bytes 10485818
  692.5 9.6 %fusion.4 = bf16[1024,2048]{1,0:T(8,128)(2,1)} fusion(bf16[1024,2048]{1,0:T(8,128)(2,1)} %get-tuple-element.75, bf16[1024,2048]{1,0:T(8,128)(2,1)} %get-tuple-element.73, s32[]{:T(128)S(6)} %select_n.55), kind=kOutput, calls=%fused_computation.6 | convolution fusion | flops 4294967296 | bytes 10485764 | tf_op jit(solution)/shard_map/cond/branch_0_fun/dot_general | solution.py:181
  702.6 6.1 conditional.15
  702.8 5.9 fusion.20
  711.2 11.0 %conditional.12 = (f32[1024,2048]{1,0:T(8,128)}) conditional(s32[]{:T(128)} %clamp.2, (s32[]{:T(128)}, bf16[1024,2048]{1,0:T(8,128)(2,1)}, bf16[1024,2048]{1,0:T(8,128)(2,1)}) %tuple.86, (s32[]{:T(128)}, bf16[1024,2048]{1,0:T(8,128)(2,1)}, bf16[1024,2048]{1,0:T(8,128)(2,1)}) %tuple.44), branch_computations={%region_9.11_spmd, %region_10.12_spmd} | conditional | flops 4299161600 | bytes 14680122 | solution.py:213
  711.4 10.8 %convert_convert_fusion = f32[1024,2048]{1,0:T(8,128)} fusion(bf16[1024,2048]{1,0:T(8,128)(2,1)} %get-tuple-element.69, bf16[1024,2048]{1,0:T(8,128)(2,1)} %get-tuple-element.67, s32[]{:T(128)S(6)} %select_n.53), kind=kOutput, calls=%fused_computation | convolution fusion | flops 4299161600 | bytes 14680068 | tf_op jit(solution)/shard_map/cond/branch_0_fun/dot_general | solution.py:181
  722.2 6.9 conditional.14
  722.4 6.5 fusion.10
  729.1 5.1 add_convert_fusion.1
  742.5 39.5 %reduce-scatter.11.cloned.1.call-done = bf16[128,2048]{1,0:T(8,128)(2,1)} async-done(((bf16[1024,2048]{1,0:T(8,128)(2,1)}), bf16[128,2048]{1,0:T(8,128)(2,1)}) %reduce-scatter.11.cloned.1.call-update) | async-done | bytes 524304 | tf_op jit(solution)/shard_map/reduce_scatter | solution.py:85
  (185 shorter events, 101.8 us)
Async XLA Ops:
  7.2 19.0 %collective-permute-start.15 = (bf16[128,2048]{1,0:T(8,128)(2,1)}, bf16[128,2048]{1,0:T(8,128)(2,1)S(1)}, u32[]{:S(2)}, u32[]{:S(2)}) collective-permute-start(bf16[128,2048]{1,0:T(8,128)(2,1)} %bitcast.82), channel_id=1, source_target_pairs={{0,2},{2,4},{4,6},{6,8},{8,10},{10,12},{12,14},{14,0},{1,3},{3,5},... | collective-permute-start | bytes 1572872 | tf_op jit(solution)/shard_map/ppermute | solution.py:16
  12.7 43.7 %collective-permute-start = (bf16[128,2048]{1,0:T(8,128)(2,1)S(1)}, bf16[128,2048]{1,0:T(8,128)(2,1)S(1)}, u32[]{:S(2)}, u32[]{:S(2)}) collective-permute-start(bf16[128,2048]{1,0:T(8,128)(2,1)S(1)} %fusion.70), channel_id=1, source_target_pairs={{0,2},{2,4},{4,6},{6,8},{8,10},{10,12},{12,14},{14,0},{1,3},{3,5},... | collective-permute-start | bytes 1572872 | tf_op jit(solution)/shard_map/ppermute | solution.py:16
  26.2 41.4 %collective-permute-start.16 = (bf16[128,2048]{1,0:T(8,128)(2,1)S(1)}, bf16[128,2048]{1,0:T(8,128)(2,1)S(1)}, u32[]{:S(2)}, u32[]{:S(2)}) collective-permute-start(bf16[128,2048]{1,0:T(8,128)(2,1)S(1)} %collective-permute-done.15), channel_id=1, source_target_pairs={{0,2},{2,4},{4,6},{6,8},{8,10},{10,12},{12,14},{14,0},{1,3},{3,5},... | collective-permute-start | bytes 1572872 | tf_op jit(solution)/shard_map/ppermute | solution.py:16
  26.2 50.5 %collective-permute-start.19 = (bf16[128,2048]{1,0:T(8,128)(2,1)}, bf16[128,2048]{1,0:T(8,128)(2,1)S(1)}, u32[]{:S(2)}, u32[]{:S(2)}) collective-permute-start(bf16[128,2048]{1,0:T(8,128)(2,1)} %bitcast.83), channel_id=1, source_target_pairs={{0,14},{2,0},{4,2},{6,4},{8,6},{10,8},{12,10},{14,12},{1,15},{3,1}... | collective-permute-start | bytes 1572872 | tf_op jit(solution)/shard_map/ppermute | solution.py:18
  30.9 62.0 %collective-permute-start.4 = (bf16[128,2048]{1,0:T(8,128)(2,1)S(1)}, bf16[128,2048]{1,0:T(8,128)(2,1)S(1)}, u32[]{:S(2)}, u32[]{:S(2)}) collective-permute-start(bf16[128,2048]{1,0:T(8,128)(2,1)S(1)} %fusion.70), channel_id=1, source_target_pairs={{0,14},{2,0},{4,2},{6,4},{8,6},{10,8},{12,10},{14,12},{1,15},{3,1}... | collective-permute-start | bytes 1572872 | tf_op jit(solution)/shard_map/ppermute | solution.py:18
  56.4 37.2 %collective-permute-start.1 = (bf16[128,2048]{1,0:T(8,128)(2,1)S(1)}, bf16[128,2048]{1,0:T(8,128)(2,1)}, u32[]{:S(2)}, u32[]{:S(2)}) collective-permute-start(bf16[128,2048]{1,0:T(8,128)(2,1)S(1)} %collective-permute-done), channel_id=1, source_target_pairs={{0,2},{2,4},{4,6},{6,8},{8,10},{10,12},{12,14},{14,0},{1,3},{3,5},... | collective-permute-start | bytes 1572872 | tf_op jit(solution)/shard_map/ppermute | solution.py:16
  67.6 53.6 %copy-start.29 = (bf16[128,2048]{1,0:T(8,128)(2,1)}, bf16[128,2048]{1,0:T(8,128)(2,1)S(1)}, u32[]{:S(2)}) copy-start(bf16[128,2048]{1,0:T(8,128)(2,1)S(1)} %collective-permute-done.16) | copy-start | bytes 1572868
  67.7 45.0 %collective-permute-start.17 = (bf16[128,2048]{1,0:T(8,128)(2,1)S(1)}, bf16[128,2048]{1,0:T(8,128)(2,1)}, u32[]{:S(2)}, u32[]{:S(2)}) collective-permute-start(bf16[128,2048]{1,0:T(8,128)(2,1)S(1)} %collective-permute-done.16), channel_id=1, source_target_pairs={{0,2},{2,4},{4,6},{6,8},{8,10},{10,12},{12,14},{14,0},{1,3},{3,5},... | collective-permute-start | bytes 1572872 | tf_op jit(solution)/shard_map/ppermute | solution.py:16
  71.8 49.5 %all-to-all-start = ((f32[8,1,256]{2,1,0:T(1,128)}), f32[8,1,256]{2,1,0:T(1,128)S(1)}, u32[]{:S(2)}, u32[]{:S(2)}) async-start(f32[8,1,256]{2,1,0:T(1,128)} %reshape.77), calls=%async_computation | async-start | bytes 16384 | tf_op jit(solution)/shard_map/all_to_all | solution.py:45
  76.7 218.5 %reduce-scatter.5.cloned.1.call-start = ((), (), s32[]{:S(2)}) async-start(), calls=%async_computation.5 | async-start | bytes 4718592 | tf_op jit(solution)/shard_map/reduce_scatter | solution.py:85
  76.7 48.7 %collective-permute-start.20 = (bf16[128,2048]{1,0:T(8,128)(2,1)S(1)}, bf16[128,2048]{1,0:T(8,128)(2,1)}, u32[]{:S(2)}, u32[]{:S(2)}) collective-permute-start(bf16[128,2048]{1,0:T(8,128)(2,1)S(1)} %collective-permute-done.19), channel_id=1, source_target_pairs={{0,14},{2,0},{4,2},{6,4},{8,6},{10,8},{12,10},{14,12},{1,15},{3,1}... | collective-permute-start | bytes 1572872 | tf_op jit(solution)/shard_map/ppermute | solution.py:18
  92.9 45.1 %collective-permute-start.5 = (bf16[128,2048]{1,0:T(8,128)(2,1)S(1)}, bf16[128,2048]{1,0:T(8,128)(2,1)}, u32[]{:S(2)}, u32[]{:S(2)}) collective-permute-start(bf16[128,2048]{1,0:T(8,128)(2,1)S(1)} %collective-permute-done.4), channel_id=1, source_target_pairs={{0,14},{2,0},{4,2},{6,4},{8,6},{10,8},{12,10},{14,12},{1,15},{3,1}... | collective-permute-start | bytes 1572872 | tf_op jit(solution)/shard_map/ppermute | solution.py:18
  93.6 45.0 %collective-permute-start.2 = (bf16[128,2048]{1,0:T(8,128)(2,1)}, bf16[128,2048]{1,0:T(8,128)(2,1)}, u32[]{:S(2)}, u32[]{:S(2)}) collective-permute-start(bf16[128,2048]{1,0:T(8,128)(2,1)} %collective-permute-done.1), channel_id=1, source_target_pairs={{0,2},{2,4},{4,6},{6,8},{8,10},{10,12},{12,14},{14,0},{1,3},{3,5},... | collective-permute-start | bytes 1572872 | tf_op jit(solution)/shard_map/ppermute | solution.py:16
  112.7 45.1 %collective-permute-start.18 = (bf16[128,2048]{1,0:T(8,128)(2,1)}, bf16[128,2048]{1,0:T(8,128)(2,1)}, u32[]{:S(2)}, u32[]{:S(2)}) collective-permute-start(bf16[128,2048]{1,0:T(8,128)(2,1)} %collective-permute-done.17), channel_id=1, source_target_pairs={{0,2},{2,4},{4,6},{6,8},{8,10},{10,12},{12,14},{14,0},{1,3},{3,5},... | collective-permute-start | bytes 1572872 | tf_op jit(solution)/shard_map/ppermute | solution.py:16
  125.4 68.6 %copy-start = (f32[128,8,2,512]{3,1,2,0:T(8,128)}, f32[128,8,2,512]{3,1,2,0:T(8,128)S(1)}, u32[]{:S(2)}) copy-start(f32[128,8,2,512]{3,1,2,0:T(8,128)S(1)} %copy.35) | copy-start | bytes 12582916
  125.4 47.0 %collective-permute-start.21 = (bf16[128,2048]{1,0:T(8,128)(2,1)}, bf16[128,2048]{1,0:T(8,128)(2,1)S(1)}, u32[]{:S(2)}, u32[]{:S(2)}) collective-permute-start(bf16[128,2048]{1,0:T(8,128)(2,1)} %collective-permute-done.20), channel_id=1, source_target_pairs={{0,14},{2,0},{4,2},{6,4},{8,6},{10,8},{12,10},{14,12},{1,15},{3,1}... | collective-permute-start | bytes 1572872 | tf_op jit(solution)/shard_map/ppermute | solution.py:18
  138.0 34.5 %collective-permute-start.6 = (bf16[128,2048]{1,0:T(8,128)(2,1)}, bf16[128,2048]{1,0:T(8,128)(2,1)S(1)}, u32[]{:S(2)}, u32[]{:S(2)}) collective-permute-start(bf16[128,2048]{1,0:T(8,128)(2,1)} %collective-permute-done.5), channel_id=1, source_target_pairs={{0,14},{2,0},{4,2},{6,4},{8,6},{10,8},{12,10},{14,12},{1,15},{3,1}... | collective-permute-start | bytes 1572872 | tf_op jit(solution)/shard_map/ppermute | solution.py:18
  138.6 29.2 %collective-permute-start.3 = (bf16[128,2048]{1,0:T(8,128)(2,1)}, bf16[128,2048]{1,0:T(8,128)(2,1)S(1)}, u32[]{:S(2)}, u32[]{:S(2)}) collective-permute-start(bf16[128,2048]{1,0:T(8,128)(2,1)} %collective-permute-done.2), channel_id=1, source_target_pairs={{0,2},{2,4},{4,6},{6,8},{8,10},{10,12},{12,14},{14,0},{1,3},{3,5},... | collective-permute-start | bytes 1572872 | tf_op jit(solution)/shard_map/ppermute | solution.py:16
  204.6 90.6 %copy-start.3 = (bf16[8,16,2048]{2,1,0:T(8,128)(2,1)S(1)}, bf16[8,16,2048]{2,1,0:T(8,128)(2,1)}, u32[]{:S(2)}) copy-start(bf16[8,16,2048]{2,1,0:T(8,128)(2,1)} %param.18) | copy-start | bytes 1572868
  204.6 106.2 %copy-start.31 = (f32[1,2048]{1,0:T(1,128)S(1)}, f32[1,2048]{1,0:T(1,128)}, u32[]{:S(2)}) copy-start(f32[1,2048]{1,0:T(1,128)} %param.22) | copy-start | bytes 24580
  204.6 330.3 %reduce-scatter.9.cloned.1.call-start = ((), (), s32[]{:S(2)}) async-start(), calls=%async_computation.7 | async-start | bytes 4718592 | tf_op jit(solution)/shard_map/reduce_scatter | solution.py:85
  296.4 98.6 %copy-start.13 = (bf16[128,2048]{1,0:T(8,128)(2,1)}, bf16[128,2048]{1,0:T(8,128)(2,1)S(1)}, u32[]{:S(2)}) copy-start(bf16[128,2048]{1,0:T(8,128)(2,1)S(1)} %fusion.77) | copy-start | bytes 1572868
  296.4 14.2 %collective-permute-start.7 = (bf16[128,2048]{1,0:T(8,128)(2,1)S(1)}, bf16[128,2048]{1,0:T(8,128)(2,1)S(1)}, u32[]{:S(2)}, u32[]{:S(2)}) collective-permute-start(bf16[128,2048]{1,0:T(8,128)(2,1)S(1)} %fusion.77), channel_id=1, source_target_pairs={{0,16},{1,17},{2,18},{3,19},{4,20},{5,21},{6,22},{7,23},{8,24},{9,... | collective-permute-start | bytes 1572872 | tf_op jit(solution)/shard_map/ppermute | solution.py:29
  310.9 15.2 %collective-permute-start.8 = (bf16[128,2048]{1,0:T(8,128)(2,1)S(1)}, bf16[128,2048]{1,0:T(8,128)(2,1)S(1)}, u32[]{:S(2)}, u32[]{:S(2)}) collective-permute-start(bf16[128,2048]{1,0:T(8,128)(2,1)S(1)} %fusion.59), channel_id=1, source_target_pairs={{0,2},{2,4},{4,6},{6,8},{8,10},{10,12},{12,14},{14,0},{1,3},{3,5},... | collective-permute-start | bytes 1572872 | tf_op jit(solution)/shard_map/ppermute | solution.py:16
  326.1 20.6 %collective-permute-start.9 = (bf16[128,2048]{1,0:T(8,128)(2,1)S(1)}, bf16[128,2048]{1,0:T(8,128)(2,1)S(1)}, u32[]{:S(2)}, u32[]{:S(2)}) collective-permute-start(bf16[128,2048]{1,0:T(8,128)(2,1)S(1)} %collective-permute-done.8), channel_id=1, source_target_pairs={{0,2},{2,4},{4,6},{6,8},{8,10},{10,12},{12,14},{14,0},{1,3},{3,5},... | collective-permute-start | bytes 1572872 | tf_op jit(solution)/shard_map/ppermute | solution.py:16
  326.1 23.6 %collective-permute-start.12 = (bf16[128,2048]{1,0:T(8,128)(2,1)S(1)}, bf16[128,2048]{1,0:T(8,128)(2,1)S(1)}, u32[]{:S(2)}, u32[]{:S(2)}) collective-permute-start(bf16[128,2048]{1,0:T(8,128)(2,1)S(1)} %fusion.59), channel_id=1, source_target_pairs={{0,14},{2,0},{4,2},{6,4},{8,6},{10,8},{12,10},{14,12},{1,15},{3,1}... | collective-permute-start | bytes 1572872 | tf_op jit(solution)/shard_map/ppermute | solution.py:18
  346.7 24.0 %collective-permute-start.10 = (bf16[128,2048]{1,0:T(8,128)(2,1)S(1)}, bf16[128,2048]{1,0:T(8,128)(2,1)S(1)}, u32[]{:S(2)}, u32[]{:S(2)}) collective-permute-start(bf16[128,2048]{1,0:T(8,128)(2,1)S(1)} %collective-permute-done.9), channel_id=1, source_target_pairs={{0,2},{2,4},{4,6},{6,8},{8,10},{10,12},{12,14},{14,0},{1,3},{3,5},... | collective-permute-start | bytes 1572872 | tf_op jit(solution)/shard_map/ppermute | solution.py:16
  349.8 23.7 %collective-permute-start.13 = (bf16[128,2048]{1,0:T(8,128)(2,1)S(1)}, bf16[128,2048]{1,0:T(8,128)(2,1)S(1)}, u32[]{:S(2)}, u32[]{:S(2)}) collective-permute-start(bf16[128,2048]{1,0:T(8,128)(2,1)S(1)} %collective-permute-done.12), channel_id=1, source_target_pairs={{0,14},{2,0},{4,2},{6,4},{8,6},{10,8},{12,10},{14,12},{1,15},{3,1}... | collective-permute-start | bytes 1572872 | tf_op jit(solution)/shard_map/ppermute | solution.py:18
  370.7 23.8 %collective-permute-start.11 = (bf16[128,2048]{1,0:T(8,128)(2,1)S(1)}, bf16[128,2048]{1,0:T(8,128)(2,1)S(1)}, u32[]{:S(2)}, u32[]{:S(2)}) collective-permute-start(bf16[128,2048]{1,0:T(8,128)(2,1)S(1)} %collective-permute-done.10), channel_id=1, source_target_pairs={{0,2},{2,4},{4,6},{6,8},{8,10},{10,12},{12,14},{14,0},{1,3},{3,5},... | collective-permute-start | bytes 1572872 | tf_op jit(solution)/shard_map/ppermute | solution.py:16
  373.5 24.2 %collective-permute-start.14 = (bf16[128,2048]{1,0:T(8,128)(2,1)S(1)}, bf16[128,2048]{1,0:T(8,128)(2,1)S(1)}, u32[]{:S(2)}, u32[]{:S(2)}) collective-permute-start(bf16[128,2048]{1,0:T(8,128)(2,1)S(1)} %collective-permute-done.13), channel_id=1, source_target_pairs={{0,14},{2,0},{4,2},{6,4},{8,6},{10,8},{12,10},{14,12},{1,15},{3,1}... | collective-permute-start | bytes 1572872 | tf_op jit(solution)/shard_map/ppermute | solution.py:18
  428.9 125.6 %copy-start.15 = (bf16[1024,1024]{1,0:T(8,128)(2,1)}, bf16[1024,1024]{1,0:T(8,128)(2,1)S(1)}, u32[]{:S(2)}) copy-start(bf16[1024,1024]{1,0:T(8,128)(2,1)S(1)} %get-tuple-element.112) | copy-start | bytes 6291460
  443.6 92.8 %copy-start.17 = (bf16[8,16,2048]{2,1,0:T(8,128)(2,1)S(1)}, bf16[8,16,2048]{2,1,0:T(8,128)(2,1)}, u32[]{:S(2)}) copy-start(bf16[8,16,2048]{2,1,0:T(8,128)(2,1)} %param.19) | copy-start | bytes 1572868
  443.6 265.6 %reduce-scatter.7.cloned.1.call-start = ((), (), s32[]{:S(2)}) async-start(), calls=%async_computation.6 | async-start | bytes 4718592 | tf_op jit(solution)/shard_map/reduce_scatter | solution.py:85
  537.8 15.2 %collective-permute-start.22 = (bf16[128,2048]{1,0:T(8,128)(2,1)S(1)}, bf16[128,2048]{1,0:T(8,128)(2,1)S(1)}, u32[]{:S(2)}, u32[]{:S(2)}) collective-permute-start(bf16[128,2048]{1,0:T(8,128)(2,1)S(1)} %fusion.64), channel_id=1, source_target_pairs={{16,0},{17,1},{18,2},{19,3},{20,4},{21,5},{22,6},{23,7},{24,8},{25... | collective-permute-start | bytes 1572872 | tf_op jit(solution)/shard_map/ppermute | solution.py:29
  553.0 101.6 %copy-start.18 = (bf16[128,2048]{1,0:T(8,128)(2,1)}, bf16[128,2048]{1,0:T(8,128)(2,1)S(1)}, u32[]{:S(2)}) copy-start(bf16[128,2048]{1,0:T(8,128)(2,1)S(1)} %collective-permute-done.22) | copy-start | bytes 1572868
  553.0 15.2 %collective-permute-start.23 = (bf16[128,2048]{1,0:T(8,128)(2,1)S(1)}, bf16[128,2048]{1,0:T(8,128)(2,1)}, u32[]{:S(2)}, u32[]{:S(2)}) collective-permute-start(bf16[128,2048]{1,0:T(8,128)(2,1)S(1)} %collective-permute-done.22), channel_id=1, source_target_pairs={{0,2},{2,4},{4,6},{6,8},{8,10},{10,12},{12,14},{14,0},{1,3},{3,5},... | collective-permute-start | bytes 1572872 | tf_op jit(solution)/shard_map/ppermute | solution.py:16
  562.8 219.2 %reduce-scatter.11.cloned.1.call-start = ((), (), s32[]{:S(2)}) async-start(), calls=%async_computation.8 | async-start | bytes 4718592 | tf_op jit(solution)/shard_map/reduce_scatter | solution.py:85
  568.2 26.5 %collective-permute-start.24 = (bf16[128,2048]{1,0:T(8,128)(2,1)}, bf16[128,2048]{1,0:T(8,128)(2,1)S(1)}, u32[]{:S(2)}, u32[]{:S(2)}) collective-permute-start(bf16[128,2048]{1,0:T(8,128)(2,1)} %collective-permute-done.23), channel_id=1, source_target_pairs={{0,2},{2,4},{4,6},{6,8},{8,10},{10,12},{12,14},{14,0},{1,3},{3,5},... | collective-permute-start | bytes 1572872 | tf_op jit(solution)/shard_map/ppermute | solution.py:16
  568.2 28.9 %collective-permute-start.27 = (bf16[128,2048]{1,0:T(8,128)(2,1)S(1)}, bf16[128,2048]{1,0:T(8,128)(2,1)S(1)}, u32[]{:S(2)}, u32[]{:S(2)}) collective-permute-start(bf16[128,2048]{1,0:T(8,128)(2,1)S(1)} %collective-permute-done.22), channel_id=1, source_target_pairs={{0,14},{2,0},{4,2},{6,4},{8,6},{10,8},{12,10},{14,12},{1,15},{3,1}... | collective-permute-start | bytes 1572872 | tf_op jit(solution)/shard_map/ppermute | solution.py:18
  594.7 29.1 %collective-permute-start.25 = (bf16[128,2048]{1,0:T(8,128)(2,1)S(1)}, bf16[128,2048]{1,0:T(8,128)(2,1)S(1)}, u32[]{:S(2)}, u32[]{:S(2)}) collective-permute-start(bf16[128,2048]{1,0:T(8,128)(2,1)S(1)} %collective-permute-done.24), channel_id=1, source_target_pairs={{0,2},{2,4},{4,6},{6,8},{8,10},{10,12},{12,14},{14,0},{1,3},{3,5},... | collective-permute-start | bytes 1572872 | tf_op jit(solution)/shard_map/ppermute | solution.py:16
  597.1 29.2 %collective-permute-start.28 = (bf16[128,2048]{1,0:T(8,128)(2,1)S(1)}, bf16[128,2048]{1,0:T(8,128)(2,1)S(1)}, u32[]{:S(2)}, u32[]{:S(2)}) collective-permute-start(bf16[128,2048]{1,0:T(8,128)(2,1)S(1)} %collective-permute-done.27), channel_id=1, source_target_pairs={{0,14},{2,0},{4,2},{6,4},{8,6},{10,8},{12,10},{14,12},{1,15},{3,1}... | collective-permute-start | bytes 1572872 | tf_op jit(solution)/shard_map/ppermute | solution.py:18
  623.8 29.5 %collective-permute-start.26 = (bf16[128,2048]{1,0:T(8,128)(2,1)S(1)}, bf16[128,2048]{1,0:T(8,128)(2,1)S(1)}, u32[]{:S(2)}, u32[]{:S(2)}) collective-permute-start(bf16[128,2048]{1,0:T(8,128)(2,1)S(1)} %collective-permute-done.25), channel_id=1, source_target_pairs={{0,2},{2,4},{4,6},{6,8},{8,10},{10,12},{12,14},{14,0},{1,3},{3,5},... | collective-permute-start | bytes 1572872 | tf_op jit(solution)/shard_map/ppermute | solution.py:16
  626.3 28.6 %collective-permute-start.29 = (bf16[128,2048]{1,0:T(8,128)(2,1)S(1)}, bf16[128,2048]{1,0:T(8,128)(2,1)S(1)}, u32[]{:S(2)}, u32[]{:S(2)}) collective-permute-start(bf16[128,2048]{1,0:T(8,128)(2,1)S(1)} %collective-permute-done.28), channel_id=1, source_target_pairs={{0,14},{2,0},{4,2},{6,4},{8,6},{10,8},{12,10},{14,12},{1,15},{3,1}... | collective-permute-start | bytes 1572872 | tf_op jit(solution)/shard_map/ppermute | solution.py:18
  702.5 31.7 %collective-permute-start.30 = (bf16[1024,2048]{1,0:T(8,128)(2,1)}, bf16[1024,2048]{1,0:T(8,128)(2,1)}, u32[]{:S(2)}, u32[]{:S(2)}) collective-permute-start(bf16[1024,2048]{1,0:T(8,128)(2,1)} %get-tuple-element.122), channel_id=1, source_target_pairs={{0,1},{1,0},{2,3},{3,2},{4,5},{5,4},{6,7},{7,6},{8,9},{9,8},{10,11... | collective-permute-start | bytes 12582920 | tf_op jit(solution)/shard_map/ppermute | solution.py:237
  708.7 20.4 %collective-permute-start.31 = (bf16[512,2048]{1,0:T(8,128)(2,1)}, bf16[512,2048]{1,0:T(8,128)(2,1)}, u32[]{:S(2)}, u32[]{:S(2)}) collective-permute-start(bf16[512,2048]{1,0:T(8,128)(2,1)} %get-tuple-element.124), channel_id=1, source_target_pairs={{0,1},{1,0},{2,3},{3,2},{4,5},{5,4},{6,7},{7,6},{8,9},{9,8},{10,11... | collective-permute-start | bytes 6291464 | tf_op jit(solution)/shard_map/ppermute | solution.py:237
  739.4 42.6 %copy-start.4 = (bf16[8,16,2048]{2,1,0:T(8,128)(2,1)S(1)}, bf16[8,16,2048]{2,1,0:T(8,128)(2,1)}, u32[]{:S(2)}) copy-start(bf16[8,16,2048]{2,1,0:T(8,128)(2,1)} %param.18) | copy-start | bytes 1572868
  739.5 43.9 %copy-start.19 = (bf16[128,2048]{1,0:T(8,128)(2,1)S(1)}, bf16[128,2048]{1,0:T(8,128)(2,1)}, u32[]{:S(2)}) copy-start(bf16[128,2048]{1,0:T(8,128)(2,1)} %copy-done.18) | copy-start | bytes 1572868
  739.5 43.9 %copy-start.26 = (bf16[128,2048]{1,0:T(8,128)(2,1)S(1)}, bf16[128,2048]{1,0:T(8,128)(2,1)}, u32[]{:S(2)}) copy-start(bf16[128,2048]{1,0:T(8,128)(2,1)} %copy-done.25) | copy-start | bytes 1572868
  (24 other events, 254.4 us)
Sparse Core Ops, SparseCore 0:
  204.7 90.3 reduce-scatter.4
  443.7 91.1 reduce-scatter.8
  562.9 127.6 reduce-scatter.6
  694.0 87.9 reduce-scatter.10
